TPU v7x, 32 devices: a whole 2x2x4 slice. The times are simulated.
32 devices in a mesh: band: 16 (over z, y, x), member: 2 (over core).
Axes of the slice: x: 2, y: 2, z: 4, core: 2. Of those that a mesh axis runs over, the one named last changes fastest.
Arguments:
- scaled_atmosphere_field: float32 [80, 4096], P(None, 'band'), may hold values from -6 to 6
- perturbation: bfloat16 [2, 80, 4096], P('member', None, 'band'), may hold values from -6 to 6
- target: bfloat16 [2, 80, 4096], P('member', None, 'band'), may hold values from -6 to 6
- weight_map: bfloat16 [80, 4096], P(None, 'band'), may hold values from 0.01 to 10
- enc_send: int32 [16, 16, 32], P('band'), may hold values from -1 to 255, as said below
- enc_recv: int32 [16, 16, 32], P('band'), may hold values from -1 to 255, as said below
- dec_send: int32 [16, 16, 32], P('band'), may hold values from -1 to 255, as said below
- dec_recv: int32 [16, 16, 32], P('band'), may hold values from -1 to 255, as said below
- lattice_lift_matrix: bfloat16 [80, 512], replicated, may hold values from -0.625 to 0.625
- mixing_rescale_factor: float32 [512], replicated, may hold values from 0.1 to 1.9
- expand_matrix: bfloat16 [512, 512], replicated, may hold values from -0.25 to 0.25
- contract_matrix: bfloat16 [512, 512], replicated, may hold values from -0.25 to 0.25
- readout_matrix: bfloat16 [512, 80], replicated, may hold values from -0.25 to 0.25
Outputs:
- student_outputs: float32 [2, 80, 4096], P('member', None, 'band')
- mesh_grad: bfloat16 [2, 4096, 512], P('member', 'band')
- grad_up: float32 [2, 512, 512], P('member')
- grad_down: float32 [2, 512, 512], P('member')
- grad_dec: float32 [2, 512, 80], P('member')
- grad_gain: float32 [2, 512], P('member')
Inputs may be any that keep to these rules, and one draw needn't show every extreme that they name: enc_send[s, d, k] is a local grid cell of band s (0 to 255) or -1 for an empty slot; in every draw one band fills all its slots and one partition receives full blocks of 32 from every band. enc_recv[d, s, k] is a local mesh node of partition d, and -1 exactly where enc_send[s, d, k] is -1. dec_send[s, d, k] is a local mesh node of partition s or -1 for an empty slot; in every draw one partition fills all its slots and one band receives full blocks of 32 from every partition. dec_recv[d, s, k] is a local grid cell of band d, and -1 exactly where dec_send[s, d, k] is -1.
All inputs are finite; a program needn't handle non-finite values.
Results may differ from a plain program's by a relative error of at most 0.0062.
Values may be sent and summed in bfloat16 or wider, within the bound.
No kernel may reach another device: no remote copies, remote signals or barrier semaphores. Data moves between devices by JAX's collectives and lax.ppermute only.
A program may use at most 64 MiB of HBM per device.

v0:
```python
import math
import jax
import jax.numpy as jnp
from jax import lax
from jax.sharding import PartitionSpec as P

MESH_DEV = 256
smooth_sq = 0.01
norm_eps = 1e-05


def slope(diff):
    return diff * lax.rsqrt(diff * diff + smooth_sq)


def embed_columns(columns, lattice_lift_matrix):
    pre_act = lax.dot_general(
        columns, lattice_lift_matrix, (((0,), (0,)), ((), ())), preferred_element_type=jnp.float32
    )
    return jax.nn.silu(pre_act).astype(jnp.bfloat16)


def body(
    scaled_atmosphere_field,
    perturbation,
    target,
    weight_map,
    enc_send,
    enc_recv,
    dec_send,
    dec_recv,
    lattice_lift_matrix,
    mixing_rescale_factor,
    expand_matrix,
    contract_matrix,
    readout_matrix,
):
    highest = lax.Precision.HIGHEST
    band_count = lax.axis_size("band")
    channels, grid_rows = scaled_atmosphere_field.shape
    width = lattice_lift_matrix.shape[1]
    node_rows = MESH_DEV
    enc_width = enc_send.shape[2]
    dec_width = dec_send.shape[2]
    cell_ids = jnp.arange(grid_rows, dtype=jnp.int32)
    node_ids = jnp.arange(node_rows, dtype=jnp.int32)
    inputs_b = (scaled_atmosphere_field + perturbation[0].astype(jnp.float32)).astype(jnp.bfloat16)
    send_index = enc_send[0].reshape(-1)
    picker = (send_index[:, None] == cell_ids[None, :]).astype(jnp.bfloat16)
    latent = embed_columns(inputs_b, lattice_lift_matrix)
    outgoing = jnp.dot(picker, latent, preferred_element_type=jnp.float32).astype(jnp.bfloat16)
    arrived = lax.all_to_all(
        outgoing.reshape(band_count, enc_width, width),
        "band",
        split_axis=0,
        concat_axis=0,
        tiled=True,
    )
    slot_rows = arrived.reshape(-1, width)
    recv_index = enc_recv[0].reshape(-1)
    landing = (node_ids[:, None] == recv_index[None, :]).astype(jnp.bfloat16)
    summed = jnp.dot(landing, slot_rows, preferred_element_type=jnp.float32)
    edge_count = jnp.sum(landing.astype(jnp.float32), axis=1, keepdims=True)
    mesh_state = summed / jnp.maximum(edge_count, 1.0)
    recip = lax.rsqrt(jnp.mean(mesh_state * mesh_state, axis=1, keepdims=True) + norm_eps)
    normed_b = (mesh_state * recip * mixing_rescale_factor).astype(jnp.bfloat16)
    hidden_pre = jnp.dot(normed_b, expand_matrix, preferred_element_type=jnp.float32)
    hidden_b = jax.nn.silu(hidden_pre).astype(jnp.bfloat16)
    mesh_next = mesh_state + jnp.dot(hidden_b, contract_matrix, preferred_element_type=jnp.float32)
    next_b = mesh_next.astype(jnp.bfloat16)
    dec_index = dec_send[0].reshape(-1)
    mesh_picker = (dec_index[:, None] == node_ids[None, :]).astype(jnp.bfloat16)
    cell_index = dec_recv[0].reshape(-1)
    fill_map = (cell_ids[:, None] == cell_index[None, :]).astype(jnp.bfloat16)
    grid_count = jnp.sum(fill_map.astype(jnp.float32), axis=1)
    inverse = 1.0 / jnp.maximum(grid_count, 1.0)
    projected = lax.dot_general(
        readout_matrix, next_b, (((0,), (1,)), ((), ())), preferred_element_type=jnp.float32
    ).astype(jnp.bfloat16)
    chosen = lax.dot_general(
        projected, mesh_picker, (((1,), (1,)), ((), ())), preferred_element_type=jnp.float32
    ).astype(jnp.bfloat16)
    slot_values = lax.all_to_all(
        chosen.reshape(channels, band_count, dec_width),
        "band",
        split_axis=1,
        concat_axis=1,
        tiled=True,
    ).reshape(channels, -1)
    grid_sum = lax.dot_general(
        slot_values, fill_map, (((1,), (1,)), ((), ())), preferred_element_type=jnp.float32
    )
    student_outputs = scaled_atmosphere_field + grid_sum * inverse[None, :]
    all_pred, all_target = (
        lax.all_gather(student_outputs[None], "member", axis=0, tiled=True),
        lax.all_gather(target.astype(jnp.float32), "member", axis=0, tiled=True),
    )
    teacher_terms = jnp.sum(slope(student_outputs[None] - all_target), axis=0)
    own_terms = jnp.sum(slope(student_outputs[None] - all_pred), axis=0)
    pred_grad = weight_map.astype(jnp.float32) * (teacher_terms - own_terms)
    scaled = pred_grad * inverse[None, :]
    slot_grad = jnp.dot(scaled, fill_map.astype(jnp.float32), precision=highest)
    dec_f32 = readout_matrix.astype(jnp.float32)
    picker_f32 = mesh_picker.astype(jnp.float32)
    returned = lax.all_to_all(
        slot_grad.reshape(channels, band_count, dec_width),
        "band",
        split_axis=1,
        concat_axis=1,
        tiled=True,
    ).reshape(channels, -1)
    node_grad = jnp.dot(returned, picker_f32, precision=highest)
    next_grad = lax.dot_general(node_grad, dec_f32, (((0,), (1,)), ((), ())), precision=highest)
    dec_part = lax.dot_general(
        next_b.astype(jnp.float32), node_grad, (((0,), (1,)), ((), ())), precision=highest
    )
    down_part = lax.dot_general(
        hidden_b.astype(jnp.float32), next_grad, (((0,), (0,)), ((), ())), precision=highest
    )
    hidden_grad = lax.dot_general(
        next_grad, contract_matrix.astype(jnp.float32), (((1,), (1,)), ((), ())), precision=highest
    )
    sigma = jax.nn.sigmoid(hidden_pre)
    pre_grad = hidden_grad * sigma * (1.0 + hidden_pre * (1.0 - sigma))
    up_part = lax.dot_general(
        normed_b.astype(jnp.float32), pre_grad, (((0,), (0,)), ((), ())), precision=highest
    )
    normed_grad = lax.dot_general(
        pre_grad, expand_matrix.astype(jnp.float32), (((1,), (1,)), ((), ())), precision=highest
    )
    gain_part = jnp.sum(normed_grad * mesh_state * recip, axis=0)
    gained = normed_grad * mixing_rescale_factor
    state_grad = (
        next_grad
        + recip * gained
        - mesh_state
        * (recip * recip * recip)
        * jnp.mean(gained * mesh_state, axis=1, keepdims=True)
    )
    up_sum, down_sum, dec_sum, gain_sum = lax.psum(
        (up_part, down_part, dec_part, gain_part), "band"
    )
    factor = 1.0 / math.sqrt(band_count * node_rows)
    return (
        student_outputs[None],
        state_grad.astype(jnp.bfloat16)[None],
        (up_sum * factor)[None],
        (down_sum * factor)[None],
        (dec_sum * factor)[None],
        (gain_sum * factor)[None],
    )


def solution(mesh):
    return jax.shard_map(
        body,
        mesh=mesh,
        in_specs=(
            P(None, "band"),
            P("member", None, "band"),
            P("member", None, "band"),
            P(None, "band"),
            P("band", None, None),
            P("band", None, None),
            P("band", None, None),
            P("band", None, None),
            P(),
            P(),
            P(),
            P(),
            P(),
        ),
        out_specs=(
            P("member", None, "band"),
            P("member", "band", None),
            P("member", None, None),
            P("member", None, None),
            P("member", None, None),
            P("member", None),
        ),
        check_vma=False,
    )
```

profile of v0, /device:TPU:0, one launch (start us, length us, event | category | flops | bytes accessed | tf_op | source)
XLA Modules:
  0.0 213.1 jit_solution(13352040407852293177)
XLA Ops:
  7.2 0.0 copy-start
  7.2 0.8 eq.64
  8.0 2.4 %convolution_convert_fusion = bf16[512,512]{1,0:T(8,128)(2,1)} fusion(bf16[80,512]{1,0:T(8,128)(2,1)} %param.21, s32[512]{0:T(512)S(1)} %eq.64, f32[80,256]{1,0:T(8,128)} %param.13, bf16[1,80,256]{2,1,0:T(8,128)(2,1)} %param.14), kind=kOutput, calls=%fused_computation | convolution fusion | flops 156299264 | bytes 731136 | tf_op jit(solution)/shard_map/dot_general | solution.py:51
  10.4 0.0 copy-start.6
  10.4 0.0 copy-start.4
  10.4 8.5 %all-to-all-start = ((bf16[16,32,512]{2,1,0:T(8,128)(2,1)}), bf16[16,32,512]{2,1,0:T(8,128)(2,1)S(1)}, u32[]{:S(2)}, u32[]{:S(2)}) async-start(bf16[16,32,512]{2,1,0:T(8,128)(2,1)} %bitcast.1), calls=%async_computation | async-start | bytes 1048576 | tf_op jit(solution)/shard_map/all_to_all | solution.py:52
  18.8 0.0 copy-done.6
  18.9 0.0 copy-start.7
  18.9 0.0 copy-start.8
  18.9 0.1 eq.73
  19.0 0.6 copy-done.7
  19.6 0.1 eq.61
  19.6 0.0 copy-done.8
  19.6 0.1 eq.68
  19.7 0.0 copy-done.4
  19.7 1.9 all_gather.6
  21.7 0.1 convert_reduce_fusion
  21.8 0.1 convert_reduce_fusion.1
  21.9 12.0 %all-to-all-done = bf16[16,32,512]{2,1,0:T(8,128)(2,1)S(1)} async-done(((bf16[16,32,512]{2,1,0:T(8,128)(2,1)}), bf16[16,32,512]{2,1,0:T(8,128)(2,1)S(1)}, u32[]{:S(2)}, u32[]{:S(2)}) %all-to-all-start) | async-done | bytes 524320 | tf_op jit(solution)/shard_map/all_to_all | solution.py:52
  33.9 0.4 multiply_reduce_fusion.2
  34.3 0.0 copy-start.5
  34.4 0.0 copy-done
  34.4 0.7 copy-done.5
  35.0 0.0 copy-start.9
  35.0 0.3 fusion.27
  35.4 0.7 copy-done.9
  36.1 0.0 copy-start.2
  36.1 0.3 fusion.1
  36.4 0.5 copy-done.2
  37.0 0.5 convolution_convert_fusion.1
  37.4 0.8 copy.23
  38.2 0.0 copy-start.10
  38.2 4.1 %all-to-all-start.1 = ((bf16[80,16,32]{0,2,1:T(8,128)(2,1)}), bf16[80,16,32]{0,2,1:T(8,128)(2,1)S(1)}, u32[]{:S(2)}, u32[]{:S(2)}) async-start(bf16[80,16,32]{0,2,1:T(8,128)(2,1)} %bitcast.3), calls=%async_computation.1 | async-start | bytes 262144 | tf_op jit(solution)/shard_map/all_to_all | solution.py:83
  42.3 0.0 all-reduce.3.cloned.1.call-start
  42.3 7.7 %all-to-all-done.1 = bf16[80,16,32]{0,2,1:T(8,128)(2,1)S(1)} async-done(((bf16[80,16,32]{0,2,1:T(8,128)(2,1)}), bf16[80,16,32]{0,2,1:T(8,128)(2,1)S(1)}, u32[]{:S(2)}, u32[]{:S(2)}) %all-to-all-start.1) | async-done | bytes 81952 | tf_op jit(solution)/shard_map/all_to_all | solution.py:83
  50.1 0.0 copy-done.10
  50.1 0.2 fusion.2
  50.3 0.0 copy-start.1
  50.3 1.9 all-gather
  52.2 0.0 copy-done.1
  52.2 0.0 copy-start.3
  52.3 0.1 multiply_reduce_fusion.3
  52.3 0.7 copy-done.3
  53.0 0.6 fusion.3
  53.6 13.0 %all_to_all.15 = f32[80,16,32]{0,2,1:T(8,128)S(1)} all-to-all(f32[80,16,32]{0,2,1:T(8,128)S(1)} %bitcast.42), channel_id=1, replica_groups=mesh['band'=16,'member'=2] {'band'}, dimensions={1} | all-to-all | bytes 327680 | tf_op jit(solution)/shard_map/all_to_all | solution.py:105
  66.7 0.5 fusion.5
  67.2 0.9 fusion.30
  68.1 0.4 fusion.29
  68.5 0.7 fusion
  69.2 1.7 fusion.28
  70.9 1.7 fusion.26
  72.6 0.0 all-reduce.3.cloned.1.call-update
  72.7 0.7 multiply_reduce_fusion
  73.4 40.0 %psum.31 = f32[512]{0:T(512)S(1)} all-reduce(f32[512]{0:T(512)S(1)} %get-tuple-element.6), channel_id=1, replica_groups=mesh['band'=16,'member'=2] {'band'}, use_global_device_ids=true, to_apply=%region_10.11 | all-reduce | flops 512 | bytes 4096 | tf_op jit(solution)/shard_map/psum | solution.py:140
  113.4 0.6 broadcast_multiply_fusion
  114.0 0.9 fusion.7
  114.8 86.7 %all-reduce.3.cloned.1.call-done = (f32[512,512]{1,0:T(8,128)}, f32[512,512]{1,0:T(8,128)}, f32[512,80]{0,1:T(8,128)}) async-done(((f32[512,512]{1,0:T(8,128)}, f32[512,512]{1,0:T(8,128)}, f32[512,80]{0,1:T(8,128)}), (f32[512,512]{1,0:T(8,128)}, f32[512,512]{1,0:T(8,128)}, f32[512,80]{0,1:T(8,128)})) %all-reduce.3.cloned.1.call-update) | async-done | bytes 2261008 | tf_op jit(solution)/shard_map/psum | solution.py:140
  201.6 1.6 multiply_bitcast_fusion.2
  203.2 3.1 %multiply_bitcast_fusion = (f32[1,512,512]{2,1,0:T(8,128)}, f32[1,512,512]{2,1,0:T(8,128)}) fusion(f32[512,512]{1,0:T(8,128)} %get-tuple-element.11, f32[512,512]{1,0:T(8,128)} %get-tuple-element.10), kind=kLoop, calls=%fused_computation.10 | loop fusion | flops 524288 | bytes 4194304 | tf_op jit(solution)/shard_map/broadcast_in_dim | solution.py:148
  (5 shorter events, 0.0 us)
Async XLA Ops:
  7.2 27.2 %copy-start = (bf16[512,512]{1,0:T(8,128)(2,1)S(1)}, bf16[512,512]{1,0:T(8,128)(2,1)}, u32[]{:S(2)}) copy-start(bf16[512,512]{1,0:T(8,128)(2,1)} %param.23) | copy-start | bytes 1572868
  10.4 8.5 %copy-start.6 = (s32[1,16,32]{2,1,0:T(8,128)S(1)}, s32[1,16,32]{2,1,0:T(8,128)}, u32[]{:S(2)}) copy-start(s32[1,16,32]{2,1,0:T(8,128)} %param.20) | copy-start | bytes 6148
  10.4 9.3 %copy-start.4 = (bf16[1,80,256]{2,1,0:T(8,128)(2,1)S(1)}, bf16[1,80,256]{2,1,0:T(8,128)(2,1)}, u32[]{:S(2)}) copy-start(bf16[1,80,256]{2,1,0:T(8,128)(2,1)} %param.15) | copy-start | bytes 122884
  10.4 23.6 %all-to-all-start = ((bf16[16,32,512]{2,1,0:T(8,128)(2,1)}), bf16[16,32,512]{2,1,0:T(8,128)(2,1)S(1)}, u32[]{:S(2)}, u32[]{:S(2)}) async-start(bf16[16,32,512]{2,1,0:T(8,128)(2,1)} %bitcast.1), calls=%async_computation | async-start | bytes 1048576 | tf_op jit(solution)/shard_map/all_to_all | solution.py:52
  18.9 0.7 copy-start.7
  18.9 0.8 copy-start.8
  34.3 0.7 copy-start.5
  35.0 1.0 copy-start.9
  36.1 0.9 copy-start.2
  38.2 11.9 %copy-start.10 = (f32[80,256]{1,0:T(8,128)S(1)}, f32[80,256]{1,0:T(8,128)}, u32[]{:S(2)}) copy-start(f32[80,256]{1,0:T(8,128)} %param.13) | copy-start | bytes 245764
  38.2 11.9 %all-to-all-start.1 = ((bf16[80,16,32]{0,2,1:T(8,128)(2,1)}), bf16[80,16,32]{0,2,1:T(8,128)(2,1)S(1)}, u32[]{:S(2)}, u32[]{:S(2)}) async-start(bf16[80,16,32]{0,2,1:T(8,128)(2,1)} %bitcast.3), calls=%async_computation.1 | async-start | bytes 262144 | tf_op jit(solution)/shard_map/all_to_all | solution.py:83
  42.3 159.3 %all-reduce.3.cloned.1.call-start = ((), (), s32[]{:S(2)}) async-start(), calls=%async_computation.3 | async-start | bytes 4521984 | tf_op jit(solution)/shard_map/psum | solution.py:140
  50.3 1.9 copy-start.1
  52.2 0.8 copy-start.3
Sparse Core Ops, SparseCore 0:
  72.8 128.7 all-reduce.2
where the time goes:
time: 214 us; the launch traced here: 213 us
  waiting for transfers between devices  106 us (50%)
  blocking collectives  56.9 us (27%)
  between operations  14.2 us (7%)
  starting transfers between devices  12.6 us (6%)
  matrix products  11.4 us (5%)
  other arithmetic  6.51 us (3%)
  local copies, waits for them, and re-layouts  5.08 us (2%)
    psum x1, waiting for transfers between devices, body(): lax.psum((up_part, down_part, dec_part, gain_part), 'band')  86.7 us
    psum x1, blocking collectives, body(): lax.psum((up_part, down_part, dec_part, gain_part), 'band')  40 us
    all_to_all x1, blocking collectives, body(): lax.all_to_all(slot_grad.reshape(channels, band_count, dec_width), 'band'...  13 us
    all_to_all x1, waiting for transfers between devices, body(): lax.all_to_all(outgoing.reshape(band_count, enc_width, width), 'band', sp...  12 us
    all_to_all x1, starting transfers between devices, body(): lax.all_to_all(outgoing.reshape(band_count, enc_width, width), 'band', sp...  8.47 us
    all_to_all x1, waiting for transfers between devices, body(): lax.all_to_all(chosen.reshape(channels, band_count, dec_width), 'band', s...  7.73 us
  transfers between devices with their start and end apart: 3, of which 3 were waited for; matrix products, arithmetic and copies ran while one was open for 1% of the time, Pallas kernels for 0%

commit v1 on v0

--- a/solution.py
+++ b/solution.py
@@ -80,12 +80,18 @@
     chosen = lax.dot_general(
         projected, mesh_picker, (((1,), (1,)), ((), ())), preferred_element_type=jnp.float32
     ).astype(jnp.bfloat16)
-    slot_values = lax.all_to_all(
-        chosen.reshape(channels, band_count, dec_width),
-        "band",
-        split_axis=1,
-        concat_axis=1,
-        tiled=True,
+    slot_values = jnp.concatenate(
+        lax.all_to_all(
+            jnp.stack(
+                jnp.split(
+                    chosen.reshape(channels, band_count, dec_width), lax.axis_size("band"), axis=1
+                )
+            ),
+            "band",
+            0,
+            0,
+        ),
+        axis=1,
     ).reshape(channels, -1)
     grid_sum = lax.dot_general(
         slot_values, fill_map, (((1,), (1,)), ((), ())), preferred_element_type=jnp.float32

time: 214 us -> 223 us (1.042)
  local copies, waits for them, and re-layouts: 5.08 us -> 14 us
    unnamed x22 -> x37, local copies, waits for them, and re-layouts: 3.26 us -> 12.2 us
where the time goes in v1:
time: 223 us; the launch traced here: 222 us
  waiting for transfers between devices  107 us (48%)
  blocking collectives  56.9 us (26%)
  between operations  14.2 us (6%)
  local copies, waits for them, and re-layouts  14 us (6%)
  starting transfers between devices  12.6 us (6%)
  matrix products  11.4 us (5%)
  other arithmetic  6.51 us (3%)
    psum x1, waiting for transfers between devices, body(): lax.psum((up_part, down_part, dec_part, gain_part), 'band')  86.8 us
    psum x1, blocking collectives, body(): lax.psum((up_part, down_part, dec_part, gain_part), 'band')  40 us
    all_to_all x1, blocking collectives, body(): lax.all_to_all(slot_grad.reshape(channels, band_count, dec_width), 'band'...  13 us
    unnamed x37, local copies, waits for them, and re-layouts  12.2 us
    all_to_all x1, waiting for transfers between devices, body(): lax.all_to_all(outgoing.reshape(band_count, enc_width, width), 'band', sp...  12 us
    all_to_all x1, starting transfers between devices, body(): lax.all_to_all(outgoing.reshape(band_count, enc_width, width), 'band', sp...  8.47 us
    all_to_all x1, waiting for transfers between devices, body(): lax.all_to_all(jnp.stack(jnp.split(chosen.reshape(channels, band_count, d...  7.73 us
  transfers between devices with their start and end apart: 3, of which 3 were waited for; matrix products, arithmetic and copies ran while one was open for 1% of the time, Pallas kernels for 0%

profile of v1, /device:TPU:0, one launch (start us, length us, event | category | flops | bytes accessed | tf_op | source)
XLA Modules:
  0.0 222.1 jit_solution(12960877795679446161)
XLA Ops:
  7.2 0.0 copy-start
  7.2 0.8 eq.64
  8.0 2.4 %convolution_convert_fusion = bf16[512,512]{1,0:T(8,128)(2,1)} fusion(bf16[80,512]{1,0:T(8,128)(2,1)} %param.21, s32[512]{0:T(512)S(1)} %eq.64, f32[80,256]{1,0:T(8,128)} %param.13, bf16[1,80,256]{2,1,0:T(8,128)(2,1)} %param.14), kind=kOutput, calls=%fused_computation | convolution fusion | flops 156299264 | bytes 731136 | tf_op jit(solution)/shard_map/dot_general | solution.py:51
  10.4 8.5 %all-to-all-start = ((bf16[16,32,512]{2,1,0:T(8,128)(2,1)}), bf16[16,32,512]{2,1,0:T(8,128)(2,1)S(1)}, u32[]{:S(2)}, u32[]{:S(2)}) async-start(bf16[16,32,512]{2,1,0:T(8,128)(2,1)} %bitcast.1), calls=%async_computation | async-start | bytes 1048576 | tf_op jit(solution)/shard_map/all_to_all | solution.py:52
  18.9 0.0 copy-start.7
  18.9 0.0 copy-start.8
  18.9 0.1 eq.73
  19.0 0.6 copy-done.7
  19.6 0.1 eq.61
  19.6 0.1 eq.68
  19.7 0.0 copy-done.4
  19.7 1.9 all_gather.6
  21.7 0.1 convert_reduce_fusion
  21.8 0.1 convert_reduce_fusion.1
  21.9 12.0 %all-to-all-done = bf16[16,32,512]{2,1,0:T(8,128)(2,1)S(1)} async-done(((bf16[16,32,512]{2,1,0:T(8,128)(2,1)}), bf16[16,32,512]{2,1,0:T(8,128)(2,1)S(1)}, u32[]{:S(2)}, u32[]{:S(2)}) %all-to-all-start) | async-done | bytes 524320 | tf_op jit(solution)/shard_map/all_to_all | solution.py:52
  33.9 0.4 multiply_reduce_fusion.2
  34.3 0.0 copy-start.5
  34.4 0.7 copy-done.5
  35.0 0.3 fusion.27
  35.4 0.7 copy-done.9
  36.1 0.3 fusion.1
  36.4 0.5 copy-done.2
  37.0 0.5 convolution_convert_fusion.1
  37.4 0.1 copy.38
  37.5 0.6 constant_dynamic-update-slice_fusion.15
  38.2 0.6 constant_dynamic-update-slice_fusion.14
  38.8 0.6 constant_dynamic-update-slice_fusion.13
  39.4 0.6 constant_dynamic-update-slice_fusion.12
  40.0 0.6 constant_dynamic-update-slice_fusion.11
  40.6 0.6 constant_dynamic-update-slice_fusion.10
  41.1 0.6 constant_dynamic-update-slice_fusion.9
  41.7 0.6 constant_dynamic-update-slice_fusion.8
  42.3 0.6 constant_dynamic-update-slice_fusion.7
  42.9 0.6 constant_dynamic-update-slice_fusion.6
  43.5 0.6 constant_dynamic-update-slice_fusion.5
  44.1 0.6 constant_dynamic-update-slice_fusion.4
  44.7 0.6 constant_dynamic-update-slice_fusion.3
  45.3 0.6 constant_dynamic-update-slice_fusion.2
  45.9 0.6 constant_dynamic-update-slice_fusion.1
  46.5 0.6 constant_dynamic-update-slice_fusion
  47.1 4.1 %all-to-all-start.1 = ((bf16[16,80,1,32]{1,3,2,0:T(8,128)(2,1)}), bf16[16,80,1,32]{1,3,2,0:T(8,128)(2,1)S(1)}, u32[]{:S(2)}, u32[]{:S(2)}) async-start(bf16[16,80,1,32]{1,3,2,0:T(8,128)(2,1)} %constant_dynamic-update-slice_fusion), calls=%async_computation.1 | async-start | bytes 262144 | tf_op jit(solution)/shard_map/all_to_all | solution.py:84
  51.2 0.0 all-reduce.3.cloned.1.call-start
  51.3 7.7 %all-to-all-done.1 = bf16[16,80,1,32]{1,3,2,0:T(8,128)(2,1)S(1)} async-done(((bf16[16,80,1,32]{1,3,2,0:T(8,128)(2,1)}), bf16[16,80,1,32]{1,3,2,0:T(8,128)(2,1)S(1)}, u32[]{:S(2)}, u32[]{:S(2)}) %all-to-all-start.1) | async-done | bytes 81952 | tf_op jit(solution)/shard_map/all_to_all | solution.py:84
  59.0 0.2 fusion.2
  59.3 0.0 copy-start.1
  59.3 1.9 all-gather
  61.2 0.1 multiply_reduce_fusion.3
  61.3 0.7 copy-done.3
  62.0 0.6 fusion.3
  62.6 13.0 %all_to_all.15 = f32[80,16,32]{0,2,1:T(8,128)S(1)} all-to-all(f32[80,16,32]{0,2,1:T(8,128)S(1)} %bitcast.108), channel_id=1, replica_groups=mesh['band'=16,'member'=2] {'band'}, dimensions={1} | all-to-all | bytes 327680 | tf_op jit(solution)/shard_map/all_to_all | solution.py:111
  75.7 0.5 fusion.5
  76.1 0.9 fusion.30
  77.1 0.4 fusion.29
  77.5 0.7 fusion
  78.2 1.7 fusion.28
  79.9 1.7 fusion.26
  81.6 0.0 all-reduce.3.cloned.1.call-update
  81.6 0.7 multiply_reduce_fusion
  82.4 40.0 %psum.31 = f32[512]{0:T(512)S(1)} all-reduce(f32[512]{0:T(512)S(1)} %get-tuple-element.6), channel_id=1, replica_groups=mesh['band'=16,'member'=2] {'band'}, use_global_device_ids=true, to_apply=%region_10.11 | all-reduce | flops 512 | bytes 4096 | tf_op jit(solution)/shard_map/psum | solution.py:146
  122.3 0.6 broadcast_multiply_fusion
  122.9 0.9 fusion.7
  123.8 86.8 %all-reduce.3.cloned.1.call-done = (f32[512,512]{1,0:T(8,128)}, f32[512,512]{1,0:T(8,128)}, f32[512,80]{0,1:T(8,128)}) async-done(((f32[512,512]{1,0:T(8,128)}, f32[512,512]{1,0:T(8,128)}, f32[512,80]{0,1:T(8,128)}), (f32[512,512]{1,0:T(8,128)}, f32[512,512]{1,0:T(8,128)}, f32[512,80]{0,1:T(8,128)})) %all-reduce.3.cloned.1.call-update) | async-done | bytes 2261008 | tf_op jit(solution)/shard_map/psum | solution.py:146
  210.6 1.6 multiply_bitcast_fusion.2
  212.2 3.1 %multiply_bitcast_fusion = (f32[1,512,512]{2,1,0:T(8,128)}, f32[1,512,512]{2,1,0:T(8,128)}) fusion(f32[512,512]{1,0:T(8,128)} %get-tuple-element.11, f32[512,512]{1,0:T(8,128)} %get-tuple-element.10), kind=kLoop, calls=%fused_computation.10 | loop fusion | flops 524288 | bytes 4194304 | tf_op jit(solution)/shard_map/broadcast_in_dim | solution.py:154
  (16 shorter events, 0.0 us)
Async XLA Ops:
  7.2 27.2 %copy-start = (bf16[512,512]{1,0:T(8,128)(2,1)S(1)}, bf16[512,512]{1,0:T(8,128)(2,1)}, u32[]{:S(2)}) copy-start(bf16[512,512]{1,0:T(8,128)(2,1)} %param.23) | copy-start | bytes 1572868
  10.4 8.5 %copy-start.6 = (s32[1,16,32]{2,1,0:T(8,128)S(1)}, s32[1,16,32]{2,1,0:T(8,128)}, u32[]{:S(2)}) copy-start(s32[1,16,32]{2,1,0:T(8,128)} %param.20) | copy-start | bytes 6148
  10.4 9.3 %copy-start.4 = (bf16[1,80,256]{2,1,0:T(8,128)(2,1)S(1)}, bf16[1,80,256]{2,1,0:T(8,128)(2,1)}, u32[]{:S(2)}) copy-start(bf16[1,80,256]{2,1,0:T(8,128)(2,1)} %param.15) | copy-start | bytes 122884
  10.4 23.6 %all-to-all-start = ((bf16[16,32,512]{2,1,0:T(8,128)(2,1)}), bf16[16,32,512]{2,1,0:T(8,128)(2,1)S(1)}, u32[]{:S(2)}, u32[]{:S(2)}) async-start(bf16[16,32,512]{2,1,0:T(8,128)(2,1)} %bitcast.1), calls=%async_computation | async-start | bytes 1048576 | tf_op jit(solution)/shard_map/all_to_all | solution.py:52
  18.9 0.7 copy-start.7
  18.9 0.8 copy-start.8
  34.3 0.7 copy-start.5
  35.0 1.0 copy-start.9
  36.1 0.9 copy-start.2
  47.1 11.9 %copy-start.10 = (f32[80,256]{1,0:T(8,128)S(1)}, f32[80,256]{1,0:T(8,128)}, u32[]{:S(2)}) copy-start(f32[80,256]{1,0:T(8,128)} %param.13) | copy-start | bytes 245764
  47.1 11.9 %all-to-all-start.1 = ((bf16[16,80,1,32]{1,3,2,0:T(8,128)(2,1)}), bf16[16,80,1,32]{1,3,2,0:T(8,128)(2,1)S(1)}, u32[]{:S(2)}, u32[]{:S(2)}) async-start(bf16[16,80,1,32]{1,3,2,0:T(8,128)(2,1)} %constant_dynamic-update-slice_fusion), calls=%async_computation.1 | async-start | bytes 262144 | tf_op jit(solution)/shard_map/all_to_all | solution.py:84
  51.2 159.4 %all-reduce.3.cloned.1.call-start = ((), (), s32[]{:S(2)}) async-start(), calls=%async_computation.3 | async-start | bytes 4521984 | tf_op jit(solution)/shard_map/psum | solution.py:146
  59.3 1.9 copy-start.1
  61.2 0.8 copy-start.3
Sparse Core Ops, SparseCore 0:
  81.7 128.8 all-reduce.2
